TPU v7x, 512 devices: a whole 4x8x8 slice. The times are simulated.
512 devices in a mesh: batch: 32 (over z_lo, y, core), gy: 4 (over z_hi), gx: 4 (over x).
Axes of the slice: x: 4, y: 8, z: 8 (z_hi: 4, z_lo: 2; z = z_hi * 2 + z_lo), core: 2. Of those that a mesh axis runs over, the one named last changes fastest.
Arguments:
- x_fine: bfloat16 [32, 32, 128, 256], P('batch', 'gy', 'gx'), may hold values from -6 to 6
- dy_fine: bfloat16 [32, 32, 128, 256], P('batch', 'gy', 'gx'), may hold values from -6 to 6
- x_coarse: bfloat16 [32, 16, 16, 1024], P('batch', 'gy', 'gx'), may hold values from -6 to 6
- dy_coarse: bfloat16 [32, 16, 16, 1024], P('batch', 'gy', 'gx'), may hold values from -6 to 6
- timestep: int32 [32], P('batch'), may hold values from 0 to 999
- fine_gain: float32 [256], replicated, may hold values from 0.5 to 2.5, as said below
- coarse_gain: float32 [1024], replicated, may hold values from 0.5 to 2.5, as said below
- fine_qkv: bfloat16 [256, 768], replicated, may hold values from -0.375 to 0.375
- fine_out: bfloat16 [256, 256], replicated, may hold values from -0.375 to 0.375
- coarse_qkv: bfloat16 [3, 1024, 1024], P(None, ('gy', 'gx')), may hold values from -0.1875 to 0.1875
- coarse_out: bfloat16 [1024, 1024], P(('gy', 'gx')), may hold values from -0.1875 to 0.1875
Outputs:
- dx_fine: bfloat16 [32, 32, 128, 256], P('batch', 'gy', 'gx')
- dx_coarse: bfloat16 [32, 16, 16, 1024], P('batch', 'gy', 'gx')
- grad_fine_qkv: bfloat16 [256, 768], replicated
- grad_fine_out: bfloat16 [256, 256], replicated
- grad_coarse_qkv: bfloat16 [3, 1024, 1024], P(None, ('gy', 'gx'))
- grad_coarse_out: bfloat16 [1024, 1024], P(('gy', 'gx'))
Inputs may be any that keep to these rules, and one draw needn't show every extreme that they name: `fine_gain`: the norm gains are positive. `coarse_gain`: the norm gains are positive.
All inputs are finite; a program needn't handle non-finite values.
Results may differ from a plain program's by a relative error of at most 0.017.
The roundings to bfloat16 on the way count: a program that leaves them out, or rounds other values in their place, can miss the bound.
Values may be sent and summed in bfloat16 or wider, within the bound.
A program may use at most 64 MiB of HBM per device.

v0:
```python
import math
import jax
import jax.numpy as jnp
from jax import lax
from jax.sharding import PartitionSpec as P

D_F = 256
H_F = 4
D_C = 1024
HD = 64
RAD = 3
eps = 1e-06
log_span = math.log(1000.0)
block_side = 8


def padded_2(array, sides, width):
    for axis, dim in sides:
        peers, length = (lax.axis_size(axis), array.shape[dim])
        up = [(i, (i + 1) % peers) for i in range(peers - 1)]
        down = [(j, i) for i, j in up]
        last = lax.slice_in_dim(array, length - width, length, axis=dim)
        leading = lax.slice_in_dim(array, 0, width, axis=dim)
        before = lax.ppermute(last, axis, up)
        after = lax.ppermute(leading, axis, down)
        array = jnp.concatenate([before, array, after], axis=dim)
    return array


def shifted(value, axis, steps):
    count = lax.axis_size(axis)
    leading, last = (max(0, -steps), min(count, count - steps))
    return lax.ppermute(value, axis, [(source, source + steps) for source in range(leading, last)])


def contract(pattern, first_op, second_op):
    return jnp.einsum(pattern, first_op, second_op, preferred_element_type=jnp.float32)


def score_scale():
    return 1.0 / math.sqrt(HD)


def time_gain(gains, step_value):
    channels = gains.shape[0]
    frequency = jnp.exp(-log_span * jnp.arange(channels, dtype=jnp.float32) / channels)
    return gains * (1.0 + 0.5 * jnp.cos(step_value.astype(jnp.float32) * frequency))


def norm_forward(source, factor):
    floats = source.astype(jnp.float32)
    inverse = lax.rsqrt(jnp.mean(floats * floats, axis=-1, keepdims=True) + eps)
    return ((floats * inverse * factor).astype(jnp.bfloat16), inverse)


def norm_backward(source, inverse, factor, upstream):
    floats = source.astype(jnp.float32)
    scaled = upstream * factor
    middle = jnp.mean(floats * scaled, axis=-1, keepdims=True)
    return (inverse * scaled - floats * inverse * inverse * inverse * middle).astype(jnp.bfloat16)


def to_tiles(planar):
    height, breadth, channels = planar.shape
    pieces = planar.reshape(
        height // block_side, block_side, breadth // block_side, block_side, channels
    )
    return pieces.transpose(0, 2, 1, 3, 4).reshape(-1, block_side * block_side, channels)


def from_tiles(blocks, height, breadth):
    channels = blocks.shape[-1]
    pieces = blocks.reshape(
        height // block_side, breadth // block_side, block_side, block_side, channels
    )
    return pieces.transpose(0, 2, 1, 3, 4).reshape(height, breadth, channels)


def windows(padded, height, breadth):
    extent = block_side + 2 * RAD
    block_rows = height // block_side
    across = breadth // block_side
    channels = padded.shape[-1]
    widened = jnp.pad(
        padded,
        (
            (0, (block_rows + 1) * block_side - padded.shape[0]),
            (0, (across + 1) * block_side - padded.shape[1]),
            (0, 0),
        ),
    )
    blocks_grid = widened.reshape(
        block_rows + 1, block_side, across + 1, block_side, channels
    ).transpose(0, 2, 1, 3, 4)
    upper_pair = jnp.concatenate([blocks_grid[:-1, :-1], blocks_grid[:-1, 1:]], axis=3)
    lower_pair = jnp.concatenate([blocks_grid[1:, :-1], blocks_grid[1:, 1:]], axis=3)
    square = jnp.concatenate([upper_pair, lower_pair], axis=2)
    return square[:, :, :extent, :extent].reshape(block_rows * across, extent * extent, channels)


def intersection_add(windowed, height, breadth):
    extent = block_side + 2 * RAD
    block_rows = height // block_side
    across = breadth // block_side
    channels = windowed.shape[-1]
    layout = windowed.reshape(block_rows, across, extent, extent, channels)
    layout = jnp.pad(
        layout, ((0, 0), (0, 0), (0, 2 * block_side - extent), (0, 2 * block_side - extent), (0, 0))
    )
    summed = jnp.zeros((block_rows + 1, across + 1, block_side, block_side, channels), jnp.float32)
    for row_half in range(2):
        for col_half in range(2):
            quarter = layout[
                :,
                :,
                row_half * block_side : (row_half + 1) * block_side,
                col_half * block_side : (col_half + 1) * block_side,
            ]
            summed = summed + jnp.pad(
                quarter,
                ((row_half, 1 - row_half), (col_half, 1 - col_half), (0, 0), (0, 0), (0, 0)),
            )
    merged = summed.transpose(0, 2, 1, 3, 4).reshape(
        (block_rows + 1) * block_side, (across + 1) * block_side, channels
    )
    return merged[: height + 2 * RAD, : breadth + 2 * RAD]


def pair_mask():
    extent = block_side + 2 * RAD
    inner_pos = jnp.arange(block_side * block_side)
    outer_pos = jnp.arange(extent * extent)
    row_gap = outer_pos[None, :] // extent - inner_pos[:, None] // block_side
    col_gap = outer_pos[None, :] % extent - inner_pos[:, None] % block_side
    return (row_gap >= 0) & (row_gap <= 2 * RAD) & (col_gap >= 0) & (col_gap <= 2 * RAD)


def fine_forward(queries, key_values, valid_pad):
    height, breadth, channels = queries.shape
    query_blocks = to_tiles(queries)
    block_count = query_blocks.shape[0]
    query_heads = query_blocks.reshape(block_count, -1, H_F, HD)
    key_windows = windows(key_values, height, breadth)
    key_heads = key_windows[..., :channels].reshape(block_count, -1, H_F, HD)
    value_heads = key_windows[..., channels:].reshape(block_count, -1, H_F, HD)
    allowed = (
        pair_mask()[None, None]
        & windows(valid_pad[..., None], height, breadth)[:, None, None, :, 0]
    )
    scores = contract("bqhe,bkhe->bhqk", query_heads, key_heads) * score_scale()
    scores = jnp.where(allowed, scores, -1e30)
    peak = jnp.max(scores, axis=-1, keepdims=True)
    log_total = peak + jnp.log(jnp.sum(jnp.exp(scores - peak), axis=-1, keepdims=True))
    shares = jnp.where(allowed, jnp.exp(scores - log_total), 0.0)
    weights = shares.astype(jnp.bfloat16)
    mixed = contract("bhqk,bkhe->bqhe", weights, value_heads).astype(jnp.bfloat16)
    attended = from_tiles(mixed.reshape(block_count, -1, channels), height, breadth)
    return (attended, query_heads, key_heads, value_heads, shares, weights, log_total)


def fine_query_backward(upstream, query_heads, key_heads, value_heads, shares, height, breadth):
    block_count = query_heads.shape[0]
    upward_heads = to_tiles(upstream).reshape(block_count, -1, H_F, HD)
    products = contract("bqhe,bkhe->bhqk", upward_heads, value_heads)
    centre = jnp.sum(shares * products, axis=-1, keepdims=True)
    slopes = (shares * (products - centre)).astype(jnp.bfloat16)
    grad_query = contract("bhqk,bkhe->bqhe", slopes, key_heads) * score_scale()
    grad_query = from_tiles(grad_query.reshape(block_count, -1, H_F * HD), height, breadth)
    return (grad_query, upward_heads, slopes, centre)


def key_grads_windows(slopes, weights, query_heads, upward_heads):
    block_count = query_heads.shape[0]
    grad_key = contract("bhqk,bqhe->bkhe", slopes, query_heads).reshape(block_count, -1, D_F)
    grad_value = contract("bhqk,bqhe->bkhe", weights, upward_heads).reshape(block_count, -1, D_F)
    return jnp.concatenate([grad_key, grad_value], axis=-1)


def local(
    x_fine,
    dy_fine,
    x_coarse,
    dy_coarse,
    timestep,
    fine_gain,
    coarse_gain,
    fine_qkv,
    fine_out,
    coarse_qkv,
    coarse_out,
):
    step_value = timestep[0]
    picture = x_fine[0]
    height, breadth = (picture.shape[0], picture.shape[1])
    factor = time_gain(fine_gain, step_value)
    normed, inverse = norm_forward(picture, factor)
    flat_normed = normed.reshape(-1, D_F)
    projected = (
        jnp.dot(flat_normed, fine_qkv, preferred_element_type=jnp.float32)
        .astype(jnp.bfloat16)
        .reshape(height, breadth, 3 * D_F)
    )
    queries = projected[..., :D_F]
    key_values = projected[..., D_F:]
    kv_pad = padded_2(key_values[None], (("gy", 1), ("gx", 2)), RAD)[0]
    row_first = lax.axis_index("gy") * height - RAD
    col_first = lax.axis_index("gx") * breadth - RAD
    pad_rows = row_first + jnp.arange(height + 2 * RAD, dtype=jnp.int32)
    pad_cols = col_first + jnp.arange(breadth + 2 * RAD, dtype=jnp.int32)
    rows_inside = (pad_rows >= 0) & (pad_rows < height * lax.axis_size("gy"))
    cols_inside = (pad_cols >= 0) & (pad_cols < breadth * lax.axis_size("gx"))
    valid_pad = rows_inside[:, None] & cols_inside[None, :]
    attended, query_heads, key_heads, value_heads, shares, weights, log_total = fine_forward(
        queries, kv_pad, valid_pad
    )
    flat_cot = dy_fine[0].reshape(-1, D_F)
    grad_out_local = lax.dot_general(
        attended.reshape(-1, D_F),
        flat_cot,
        (((0,), (0,)), ((), ())),
        preferred_element_type=jnp.float32,
    )
    upstream = (
        lax.dot_general(
            flat_cot, fine_out, (((1,), (1,)), ((), ())), preferred_element_type=jnp.float32
        )
        .astype(jnp.bfloat16)
        .reshape(height, breadth, D_F)
    )
    grad_query, upward_heads, slopes, centre = fine_query_backward(
        upstream, query_heads, key_heads, value_heads, shares, height, breadth
    )
    summed = intersection_add(
        key_grads_windows(slopes, weights, query_heads, upward_heads), height, breadth
    )
    from_left = shifted(summed[:, breadth + RAD :], "gx", 1)
    from_right = shifted(summed[:, :RAD], "gx", -1)
    middle = summed[:, RAD : breadth + RAD]
    middle = middle.at[:, :RAD].add(from_left)
    middle = middle.at[:, breadth - RAD :].add(from_right)
    from_above = shifted(middle[height + RAD :], "gy", 1)
    from_below = shifted(middle[:RAD], "gy", -1)
    key_grads = middle[RAD : height + RAD]
    key_grads = key_grads.at[:RAD].add(from_above)
    key_grads = key_grads.at[height - RAD :].add(from_below)
    grad_proj = (
        jnp.concatenate(
            [grad_query, key_grads[..., :D_F] * score_scale(), key_grads[..., D_F:]], axis=-1
        )
        .astype(jnp.bfloat16)
        .reshape(-1, 3 * D_F)
    )
    grad_qkv_local = lax.dot_general(
        flat_normed, grad_proj, (((0,), (0,)), ((), ())), preferred_element_type=jnp.float32
    )
    down_grad = lax.dot_general(
        grad_proj, fine_qkv, (((1,), (1,)), ((), ())), preferred_element_type=jnp.float32
    ).reshape(height, breadth, D_F)
    dx_picture = norm_backward(picture, inverse, factor, down_grad)
    coarse_tokens = x_coarse[0].reshape(-1, D_C)
    coarse_factor = time_gain(coarse_gain, step_value)
    coarse_normed, coarse_inverse = norm_forward(coarse_tokens, coarse_factor)
    coarse_cot = dy_coarse[0].reshape(-1, D_C)
    all_normed = lax.all_gather(coarse_normed, ("gy", "gx"), axis=0, tiled=True)
    coarse_proj = contract("td,khd->kth", all_normed, coarse_qkv).astype(jnp.bfloat16)
    head_queries, head_keys, head_values = (coarse_proj[0], coarse_proj[1], coarse_proj[2])
    coarse_scores = contract("te,se->ts", head_queries, head_keys) * score_scale()
    coarse_peak = jnp.max(coarse_scores, axis=-1, keepdims=True)
    coarse_log = coarse_peak + jnp.log(
        jnp.sum(jnp.exp(coarse_scores - coarse_peak), axis=-1, keepdims=True)
    )
    coarse_shares = jnp.exp(coarse_scores - coarse_log)
    coarse_weights = coarse_shares.astype(jnp.bfloat16)
    head_mixed = contract("ts,se->te", coarse_weights, head_values).astype(jnp.bfloat16)
    all_cot = lax.all_gather(coarse_cot, ("gy", "gx"), axis=0, tiled=True)
    head_upstream = contract("td,ed->te", all_cot, coarse_out).astype(jnp.bfloat16)
    coarse_out_local = contract("te,td->ed", head_mixed, all_cot)
    coarse_products = contract("te,se->ts", head_upstream, head_values)
    coarse_centre = jnp.sum(coarse_shares * coarse_products, axis=-1, keepdims=True)
    coarse_slopes = (coarse_shares * (coarse_products - coarse_centre)).astype(jnp.bfloat16)
    head_grad_query = (contract("ts,se->te", coarse_slopes, head_keys) * score_scale()).astype(
        jnp.bfloat16
    )
    head_grad_key = (contract("ts,te->se", coarse_slopes, head_queries) * score_scale()).astype(
        jnp.bfloat16
    )
    head_grad_value = contract("ts,te->se", coarse_weights, head_upstream).astype(jnp.bfloat16)
    stacked = jnp.stack([head_grad_query, head_grad_key, head_grad_value])
    coarse_qkv_local = contract("kte,td->ked", stacked, all_normed)
    head_part = contract("kte,ked->td", stacked, coarse_qkv)
    coarse_down = lax.psum_scatter(
        head_part.astype(jnp.bfloat16), ("gy", "gx"), scatter_dimension=0, tiled=True
    ).astype(jnp.float32)
    dx_coarse_tok = norm_backward(coarse_tokens, coarse_inverse, coarse_factor, coarse_down)
    fine_qkv_sum, fine_out_sum = lax.psum((grad_qkv_local, grad_out_local), ("batch", "gy", "gx"))
    coarse_qkv_sum, coarse_out_sum = lax.psum((coarse_qkv_local, coarse_out_local), "batch")
    return (
        dx_picture[None],
        dx_coarse_tok.reshape(x_coarse.shape),
        fine_qkv_sum.astype(jnp.bfloat16),
        fine_out_sum.astype(jnp.bfloat16),
        coarse_qkv_sum.astype(jnp.bfloat16),
        coarse_out_sum.astype(jnp.bfloat16),
    )


def solution(mesh):
    placed = (
        P("batch", "gy", "gx", None),
        P("batch", "gy", "gx", None),
        P("batch", "gy", "gx", None),
        P("batch", "gy", "gx", None),
        P("batch"),
        P(),
        P(),
        P(),
        P(),
        P(None, ("gy", "gx"), None),
        P(("gy", "gx"), None),
    )
    return jax.shard_map(
        local,
        mesh=mesh,
        in_specs=placed,
        out_specs=(
            P("batch", "gy", "gx", None),
            P("batch", "gy", "gx", None),
            P(),
            P(),
            P(None, ("gy", "gx"), None),
            P(("gy", "gx"), None),
        ),
        check_vma=False,
    )
```

profile of v0, /device:TPU:1, one launch (start us, length us, event | category | flops | bytes accessed | tf_op | source)
XLA Modules:
  0.0 400.2 jit_solution(13088266657257998717)
XLA Ops:
  11.3 1.3 convolution_convert_fusion
  12.7 6.8 %collective-permute-start = (bf16[1,3,32,512]{3,2,1,0:T(8,128)(2,1)S(1)}, bf16[1,3,32,512]{3,2,1,0:T(8,128)(2,1)S(1)}, u32[]{:S(2)}, u32[]{:S(2)}) collective-permute-start(bf16[1,3,32,512]{3,2,1,0:T(8,128)(2,1)S(1)} %get-tuple-element.74), channel_id=1, source_target_pairs={{0,4},{4,8},{8,12},{1,5},{5,9},{9,13},{2,6},{6,10},{10,14},{3,7},{... | collective-permute-start | bytes 294920 | tf_op jit(solution)/shard_map/ppermute | solution.py:24
  19.4 1.3 collective-permute-start.1
  21.1 44.2 %all_gather.6 = bf16[256,1024]{1,0:T(8,128)(2,1)S(1)} all-gather(bf16[16,1024]{1,0:T(8,128)(2,1)S(1)} %multiply_convert_fusion.2), channel_id=1, replica_groups=mesh['batch'=32,'gy'=4,'gx'=4] {'gy','gx'}, dimensions={0}, use_global_device_ids=true | all-gather | bytes 557056 | tf_op jit(solution)/shard_map/all_gather | solution.py:264
  66.0 34.0 %all_gather.7 = bf16[256,1024]{1,0:T(8,128)(2,1)S(1)} all-gather(bf16[16,1024]{1,0:T(8,128)(2,1)S(1)} %reshape_squeeze.8), channel_id=1, replica_groups=mesh['batch'=32,'gy'=4,'gx'=4] {'gy','gx'}, dimensions={0}, use_global_device_ids=true | all-gather | bytes 557056 | tf_op jit(solution)/shard_map/all_gather | solution.py:275
  101.2 1.1 fusion.1
  103.5 131.1 %all-reduce.11 = (bf16[3,64,1024]{2,1,0:T(8,128)(2,1)}, bf16[64,1024]{1,0:T(8,128)(2,1)}) all-reduce(f32[3,64,1024]{2,1,0:T(8,128)S(1)} %fusion.14, f32[64,1024]{1,0:T(8,128)S(1)} %fusion.9), channel_id=1, replica_groups=mesh['batch'=32,'gy'=4,'gx'=4] {'batch'}, use_global_device_ids=true, to_apply=%region_13.14 | all-reduce | flops 262144 | bytes 1572864 | tf_op jit(solution)/shard_map/psum | solution.py:296
  235.0 2.2 collective-permute-start.2
  237.2 1.5 collective-permute-start.3
  239.5 2.6 collective-permute-done.3
  247.8 1.3 convolution_bitcast_fusion.2
  249.5 2.0 copy.49
  251.6 1.9 concatenate.57
  253.5 1.1 copy.51
  254.6 1.9 concatenate.58
  258.7 1.0 copy.52
  260.5 2.6 collective-permute-start.4
  264.5 1.3 collective-permute-start.5
  267.2 2.9 collective-permute-done.5
  270.5 1.4 collective-permute-start.6
  272.0 1.3 collective-permute-start.7
  273.3 1.2 collective-permute-done.6
  274.6 6.9 %collective-permute-done.7 = f32[3,32,512]{2,1,0:T(8,128)S(1)} collective-permute-done((f32[3,32,512]{2,1,0:T(8,128)S(1)}, f32[3,32,512]{2,1,0:T(8,128)S(1)}, u32[]{:S(2)}, u32[]{:S(2)}) %collective-permute-start.7) | collective-permute-done | bytes 196640 | tf_op jit(solution)/shard_map/ppermute | solution.py:33
  283.8 107.2 %all-reduce.12 = (bf16[256,768]{1,0:T(8,128)(2,1)}, bf16[256,256]{1,0:T(8,128)(2,1)}) all-reduce(f32[256,768]{1,0:T(8,128)S(1)} %convolution_bitcast_fusion.3, f32[256,256]{1,0:T(8,128)S(1)} %copy-done.5), channel_id=1, replica_groups=mesh['batch'=32,'gy'=4,'gx'=4] {'batch','gy','gx'}, use_global_device_ids=true, to_apply=%region_11.12 | all-reduce | flops 262144 | bytes 1572864 | tf_op jit(solution)/shard_map/psum | solution.py:295
  (146 shorter events, 24.7 us)
Async XLA Ops:
  7.2 58.1 %copy-start = (bf16[3,64,1024]{2,1,0:T(8,128)(2,1)S(1)}, bf16[3,64,1024]{2,1,0:T(8,128)(2,1)}, u32[]{:S(2)}) copy-start(bf16[3,64,1024]{2,1,0:T(8,128)(2,1)} %param.28) | copy-start | bytes 1179652
  7.2 13.6 %copy-start.10 = (bf16[1,4,4,1024]{3,2,1,0:T(4,128)(2,1)S(1)}, bf16[1,4,4,1024]{3,2,1,0:T(4,128)(2,1)}, u32[]{:S(2)}) copy-start(bf16[1,4,4,1024]{3,2,1,0:T(4,128)(2,1)} %param.21) | copy-start | bytes 98308
  7.2 13.8 %copy-start.21 = (f32[1024]{0:T(1024)S(1)}, f32[1024]{0:T(1024)}, u32[]{:S(2)}) copy-start(f32[1024]{0:T(1024)} %param.25) | copy-start | bytes 12292
  7.2 13.8 %copy-start.16 = (bf16[1,4,4,1024]{3,2,1,0:T(4,128)(2,1)S(1)}, bf16[1,4,4,1024]{3,2,1,0:T(4,128)(2,1)}, u32[]{:S(2)}) copy-start(bf16[1,4,4,1024]{3,2,1,0:T(4,128)(2,1)} %param.22) | copy-start | bytes 98308
  7.2 383.7 %reduce-scatter.2.cloned.1.call-start = ((), (), s32[]{:S(2)}) async-start(), calls=%async_computation.1 | async-start | bytes 557056 | tf_op jit(solution)/shard_map/reduce_scatter | solution.py:291
  10.3 55.0 %copy-start.19 = (f32[256]{0:T(256)}, f32[256]{0:T(256)S(1)}, u32[]{:S(2)}) copy-start(f32[256]{0:T(256)S(1)} %add_multiply_fusion.1) | copy-start | bytes 3076
  12.7 87.4 %copy-start.11 = (bf16[64,1024]{1,0:T(8,128)(2,1)S(1)}, bf16[64,1024]{1,0:T(8,128)(2,1)}, u32[]{:S(2)}) copy-start(bf16[64,1024]{1,0:T(8,128)(2,1)} %param.29) | copy-start | bytes 393220
  12.7 222.2 %collective-permute-start = (bf16[1,3,32,512]{3,2,1,0:T(8,128)(2,1)S(1)}, bf16[1,3,32,512]{3,2,1,0:T(8,128)(2,1)S(1)}, u32[]{:S(2)}, u32[]{:S(2)}) collective-permute-start(bf16[1,3,32,512]{3,2,1,0:T(8,128)(2,1)S(1)} %get-tuple-element.74), channel_id=1, source_target_pairs={{0,4},{4,8},{8,12},{1,5},{5,9},{9,13},{2,6},{6,10},{10,14},{3,7},{... | collective-permute-start | bytes 294920 | tf_op jit(solution)/shard_map/ppermute | solution.py:24
  19.4 215.5 %collective-permute-start.1 = (bf16[1,3,32,512]{3,2,1,0:T(8,128)(2,1)S(1)}, bf16[1,3,32,512]{3,2,1,0:T(8,128)(2,1)S(1)}, u32[]{:S(2)}, u32[]{:S(2)}) collective-permute-start(bf16[1,3,32,512]{3,2,1,0:T(8,128)(2,1)S(1)} %get-tuple-element.75), channel_id=1, source_target_pairs={{4,0},{8,4},{12,8},{5,1},{9,5},{13,9},{6,2},{10,6},{14,10},{7,3},{... | collective-permute-start | bytes 294920 | tf_op jit(solution)/shard_map/ppermute | solution.py:25
  21.0 44.3 %copy-start.17 = (f32[16]{0:T(128)}, f32[16]{0:T(128)S(1)}, u32[]{:S(2)}) copy-start(f32[16]{0:T(128)S(1)} %rsqrt.26) | copy-start | bytes 196
  21.0 79.3 %copy-start.12 = (f32[1024]{0:T(1024)}, f32[1024]{0:T(1024)S(1)}, u32[]{:S(2)}) copy-start(f32[1024]{0:T(1024)S(1)} %add_multiply_fusion) | copy-start | bytes 12292
  235.0 4.5 %collective-permute-start.2 = (bf16[1,14,3,512]{3,2,1,0:T(4,128)(2,1)S(1)}, bf16[1,14,3,512]{3,2,1,0:T(4,128)(2,1)S(1)}, u32[]{:S(2)}, u32[]{:S(2)}) collective-permute-start(bf16[1,14,3,512]{3,2,1,0:T(4,128)(2,1)S(1)} %get-tuple-element.72), channel_id=1, source_target_pairs={{0,1},{1,2},{2,3},{4,5},{5,6},{6,7},{8,9},{9,10},{10,11},{12,13},{... | collective-permute-start | bytes 129032 | tf_op jit(solution)/shard_map/ppermute | solution.py:24
  237.2 4.9 %collective-permute-start.3 = (bf16[1,14,3,512]{3,2,1,0:T(4,128)(2,1)S(1)}, bf16[1,14,3,512]{3,2,1,0:T(4,128)(2,1)S(1)}, u32[]{:S(2)}, u32[]{:S(2)}) collective-permute-start(bf16[1,14,3,512]{3,2,1,0:T(4,128)(2,1)S(1)} %get-tuple-element.73), channel_id=1, source_target_pairs={{1,0},{2,1},{3,2},{5,4},{6,5},{7,6},{9,8},{10,9},{11,10},{13,12},{... | collective-permute-start | bytes 129032 | tf_op jit(solution)/shard_map/ppermute | solution.py:25
  258.7 4.3 %copy-start.7 = (bf16[1,8,32,256]{3,2,1,0:T(8,128)(2,1)S(1)}, bf16[1,8,32,256]{3,2,1,0:T(8,128)(2,1)}, u32[]{:S(2)}) copy-start(bf16[1,8,32,256]{3,2,1,0:T(8,128)(2,1)} %param.20) | copy-start | bytes 393220
  259.8 4.3 %copy-start.4 = (bf16[4,64,4,64]{1,3,2,0:T(8,128)(2,1)S(1)}, bf16[4,64,4,64]{1,3,2,0:T(8,128)(2,1)}, u32[]{:S(2)}) copy-start(bf16[4,64,4,64]{1,3,2,0:T(8,128)(2,1)} %fusion.4) | copy-start | bytes 393220
  260.5 5.4 %collective-permute-start.4 = (f32[14,3,512]{2,1,0:T(4,128)}, f32[14,3,512]{2,1,0:T(4,128)}, u32[]{:S(2)}, u32[]{:S(2)}) collective-permute-start(f32[14,3,512]{2,1,0:T(4,128)} %get-tuple-element.63), channel_id=1, source_target_pairs={{0,1},{1,2},{2,3},{4,5},{5,6},{6,7},{8,9},{9,10},{10,11},{12,13},{... | collective-permute-start | bytes 258056 | tf_op jit(solution)/shard_map/ppermute | solution.py:33
  264.5 5.5 %collective-permute-start.5 = (f32[14,3,512]{2,1,0:T(4,128)S(1)}, f32[14,3,512]{2,1,0:T(4,128)S(1)}, u32[]{:S(2)}, u32[]{:S(2)}) collective-permute-start(f32[14,3,512]{2,1,0:T(4,128)S(1)} %get-tuple-element.62), channel_id=1, source_target_pairs={{1,0},{2,1},{3,2},{5,4},{6,5},{7,6},{9,8},{10,9},{11,10},{13,12},{... | collective-permute-start | bytes 258056 | tf_op jit(solution)/shard_map/ppermute | solution.py:33
  270.5 11.2 %copy-start.3 = (bf16[1,8,32,256]{3,2,1,0:T(8,128)(2,1)S(1)}, bf16[1,8,32,256]{3,2,1,0:T(8,128)(2,1)}, u32[]{:S(2)}) copy-start(bf16[1,8,32,256]{3,2,1,0:T(8,128)(2,1)} %param.19) | copy-start | bytes 393220
  270.5 11.2 %copy-start.15 = (f32[8,32]{1,0:T(8,128)S(1)}, f32[8,32]{1,0:T(8,128)}, u32[]{:S(2)}) copy-start(f32[8,32]{1,0:T(8,128)} %copy-done.14) | copy-start | bytes 3076
  270.5 11.2 %copy-start.20 = (f32[256]{0:T(256)S(1)}, f32[256]{0:T(256)}, u32[]{:S(2)}) copy-start(f32[256]{0:T(256)} %copy-done.19) | copy-start | bytes 3076
  270.5 4.1 %collective-permute-start.6 = (f32[3,32,512]{2,1,0:T(8,128)S(1)}, f32[3,32,512]{2,1,0:T(8,128)S(1)}, u32[]{:S(2)}, u32[]{:S(2)}) collective-permute-start(f32[3,32,512]{2,1,0:T(8,128)S(1)} %get-tuple-element.65), channel_id=1, source_target_pairs={{0,4},{4,8},{8,12},{1,5},{5,9},{9,13},{2,6},{6,10},{10,14},{3,7},{... | collective-permute-start | bytes 589832 | tf_op jit(solution)/shard_map/ppermute | solution.py:33
  272.0 9.5 %collective-permute-start.7 = (f32[3,32,512]{2,1,0:T(8,128)S(1)}, f32[3,32,512]{2,1,0:T(8,128)S(1)}, u32[]{:S(2)}, u32[]{:S(2)}) collective-permute-start(f32[3,32,512]{2,1,0:T(8,128)S(1)} %get-tuple-element.64), channel_id=1, source_target_pairs={{4,0},{8,4},{12,8},{5,1},{9,5},{13,9},{6,2},{10,6},{14,10},{7,3},{... | collective-permute-start | bytes 589832 | tf_op jit(solution)/shard_map/ppermute | solution.py:33
  282.6 108.4 %copy-start.13 = (f32[1024]{0:T(1024)S(1)}, f32[1024]{0:T(1024)}, u32[]{:S(2)}) copy-start(f32[1024]{0:T(1024)} %copy-done.12) | copy-start | bytes 12292
  282.6 109.3 %copy-start.18 = (f32[16]{0:T(128)S(1)}, f32[16]{0:T(128)}, u32[]{:S(2)}) copy-start(f32[16]{0:T(128)} %copy-done.17) | copy-start | bytes 196
  (7 other events, 7.8 us)
Sparse Core Ops, SparseCore 0:
  102.5 103.7 reduce-scatter.1
where the time goes:
time: 401 us; the launch traced here: 400 us
  blocking collectives  316 us (79%)
  starting transfers between devices  18.3 us (5%)
  local copies, waits for them, and re-layouts  16.8 us (4%)
  between operations  15.5 us (4%)
  waiting for transfers between devices  13.7 us (3%)
  matrix products  10.7 us (3%)
  other arithmetic  8.66 us (2%)
    psum x1, blocking collectives, local(): lax.psum((coarse_qkv_local, coarse_out_local), 'batch')  131 us
    psum x1, blocking collectives, local(): lax.psum((grad_qkv_local, grad_out_local), ('batch', 'gy', 'gx'))  107 us
    all_gather x1, blocking collectives, local(): all_normed = lax.all_gather(coarse_normed, ('gy', 'gx'), axis=0, tiled=True)  44.2 us
    all_gather x1, blocking collectives, local(): all_cot = lax.all_gather(coarse_cot, ('gy', 'gx'), axis=0, tiled=True)  34 us
    ppermute x4, waiting for transfers between devices, shifted(): lax.ppermute(value, axis, [(source, source + steps) for source in range(l...  11 us
    ppermute x2, starting transfers between devices, padded_2(): before = lax.ppermute(last, axis, up)  8.95 us
  transfers between devices with their start and end apart: 9, of which 4 were waited for; matrix products, arithmetic and copies ran while one was open for 7% of the time, Pallas kernels for 0%

commit v1 on v0

--- a/solution.py
+++ b/solution.py
@@ -3,6 +3,7 @@
 import jax.numpy as jnp
 from jax import lax
 from jax.sharding import PartitionSpec as P
+from jax.lax import all_to_all, axis_size
 
 D_F = 256
 H_F = 4
@@ -12,6 +13,18 @@
 eps = 1e-06
 log_span = math.log(1000.0)
 block_side = 8
+
+
+def solve_tables(vec):
+    return jnp.concatenate(
+        all_to_all(
+            jnp.stack([vec for _ in range(axis_size(("gy", "gx")))], 0),
+            concat_axis=0,
+            axis_name=("gy", "gx"),
+            split_axis=0,
+        ),
+        0,
+    )
 
 
 def padded_2(array, sides, width):
@@ -272,7 +285,7 @@
     coarse_shares = jnp.exp(coarse_scores - coarse_log)
     coarse_weights = coarse_shares.astype(jnp.bfloat16)
     head_mixed = contract("ts,se->te", coarse_weights, head_values).astype(jnp.bfloat16)
-    all_cot = lax.all_gather(coarse_cot, ("gy", "gx"), axis=0, tiled=True)
+    all_cot = solve_tables(coarse_cot)
     head_upstream = contract("td,ed->te", all_cot, coarse_out).astype(jnp.bfloat16)
     coarse_out_local = contract("te,td->ed", head_mixed, all_cot)
     coarse_products = contract("te,se->ts", head_upstream, head_values)

time: 401 us -> 384 us (0.958)
  blocking collectives: 316 us -> 273 us
  starting transfers between devices: 18.3 us -> 32.6 us
  local copies, waits for them, and re-layouts: 16.8 us -> 24 us
    all_gather x1 -> x0, blocking collectives: 34 us -> none  [local(): all_cot = lax.all_gather(coarse_cot, ('gy', 'gx'), axis=0, tiled=True)]
    psum x1, blocking collectives: 131 us -> 114 us  [local(): lax.psum((coarse_qkv_local, coarse_out_local), 'batch')]
    all_to_all x0 -> x1, starting transfers between devices: none -> 13 us  [solve_tables(): all_to_all(jnp.stack([vec for _ in range(axis_size(('gy', 'gx')))], 0), c...]
    psum x1, blocking collectives: 107 us -> 117 us  [local(): lax.psum((grad_qkv_local, grad_out_local), ('batch', 'gy', 'gx'))]
  transfers between devices with their start and end apart: 9 -> 10, of which waited for: 4 -> 4; matrix products, arithmetic and copies ran while one was open for 7% -> 9% of each run, Pallas kernels for 0% -> 0%
where the time goes in v1:
time: 384 us; the launch traced here: 379 us
  blocking collectives  273 us (71%)
  starting transfers between devices  32.6 us (8%)
  local copies, waits for them, and re-layouts  24 us (6%)
  between operations  15.5 us (4%)
  waiting for transfers between devices  12.4 us (3%)
  matrix products  11.8 us (3%)
  other arithmetic  10.2 us (3%)
    psum x1, blocking collectives, local(): lax.psum((grad_qkv_local, grad_out_local), ('batch', 'gy', 'gx'))  117 us
    psum x1, blocking collectives, local(): lax.psum((coarse_qkv_local, coarse_out_local), 'batch')  114 us
    all_gather x1, blocking collectives, local(): all_normed = lax.all_gather(coarse_normed, ('gy', 'gx'), axis=0, tiled=True)  41.1 us
    all_to_all x1, starting transfers between devices, solve_tables(): all_to_all(jnp.stack([vec for _ in range(axis_size(('gy', 'gx')))], 0), c...  13 us
    ppermute x4, waiting for transfers between devices, shifted(): lax.ppermute(value, axis, [(source, source + steps) for source in range(l...  9.24 us
    ppermute x2, starting transfers between devices, padded_2(): before = lax.ppermute(last, axis, up)  8.99 us
    dot_general x16, matrix products, contract(): jnp.einsum(pattern, first_op, second_op, preferred_element_type=jnp.float32)  8.59 us
    ppermute x4, starting transfers between devices, shifted(): lax.ppermute(value, axis, [(source, source + steps) for source in range(l...  7.97 us
  transfers between devices with their start and end apart: 10, of which 4 were waited for; matrix products, arithmetic and copies ran while one was open for 9% of the time, Pallas kernels for 0%

profile of v1, /device:TPU:1, one launch (start us, length us, event | category | flops | bytes accessed | tf_op | source)
XLA Modules:
  0.0 379.4 jit_solution(3266631963050063219)
XLA Ops:
  12.1 6.6 %collective-permute-start = (bf16[1,3,32,512]{3,2,1,0:T(8,128)(2,1)S(1)}, bf16[1,3,32,512]{3,2,1,0:T(8,128)(2,1)S(1)}, u32[]{:S(2)}, u32[]{:S(2)}) collective-permute-start(bf16[1,3,32,512]{3,2,1,0:T(8,128)(2,1)S(1)} %get-tuple-element.74), channel_id=1, source_target_pairs={{0,4},{4,8},{8,12},{1,5},{5,9},{9,13},{2,6},{6,10},{10,14},{3,7},{... | collective-permute-start | bytes 294920 | tf_op jit(solution)/shard_map/ppermute | solution.py:37
  18.7 1.3 collective-permute-start.1
  20.9 13.0 %all-to-all-start = ((bf16[16,16,1024]{2,1,0:T(8,128)(2,1)}), bf16[16,16,1024]{2,1,0:T(8,128)(2,1)S(1)}, u32[]{:S(2)}, u32[]{:S(2)}) async-start(bf16[16,16,1024]{2,1,0:T(8,128)(2,1)} %stack.15), calls=%async_computation | async-start | bytes 1048576 | tf_op jit(solution)/shard_map/all_to_all | solution.py:20
  34.8 41.1 %all_gather.3 = bf16[256,1024]{1,0:T(8,128)(2,1)S(1)} all-gather(bf16[16,1024]{1,0:T(8,128)(2,1)S(1)} %multiply_convert_fusion.2), channel_id=1, replica_groups=mesh['batch'=32,'gy'=4,'gx'=4] {'gy','gx'}, dimensions={0}, use_global_device_ids=true | all-gather | bytes 557056 | tf_op jit(solution)/shard_map/all_gather | solution.py:277
  77.9 2.4 collective-permute-start.2
  80.2 1.3 collective-permute-start.3
  82.3 3.1 collective-permute-done.3
  89.4 1.3 convolution_bitcast_fusion.1
  92.2 1.3 convolution_bitcast_fusion.2
  94.5 2.0 copy.49
  96.6 2.0 concatenate.57
  98.6 2.0 copy.51
  100.6 1.9 concatenate.58
  102.5 1.4 constant_dynamic-update-slice_fusion.1
  106.8 2.3 collective-permute-start.4
  110.1 1.8 copy.46
  111.9 1.8 reshape_reshape.22
  115.1 1.6 slice_add_fusion.3
  117.9 1.7 collective-permute-done.5
  120.9 3.1 collective-permute-start.6
  124.2 1.3 collective-permute-start.7
  126.5 6.5 %collective-permute-done.7 = f32[3,32,512]{2,1,0:T(8,128)S(1)} collective-permute-done((f32[3,32,512]{2,1,0:T(8,128)S(1)}, f32[3,32,512]{2,1,0:T(8,128)S(1)}, u32[]{:S(2)}, u32[]{:S(2)}) %collective-permute-start.7) | collective-permute-done | bytes 196640 | tf_op jit(solution)/shard_map/ppermute | solution.py:46
  135.3 117.5 %all-reduce.12 = (bf16[256,768]{1,0:T(8,128)(2,1)}, bf16[256,256]{1,0:T(8,128)(2,1)}) all-reduce(f32[256,768]{1,0:T(8,128)S(1)} %convolution_bitcast_fusion.3, f32[256,256]{1,0:T(8,128)S(1)} %copy-done.5), channel_id=1, replica_groups=mesh['batch'=32,'gy'=4,'gx'=4] {'batch','gy','gx'}, use_global_device_ids=true, to_apply=%region_11.12 | all-reduce | flops 262144 | bytes 1572864 | tf_op jit(solution)/shard_map/psum | solution.py:308
  255.8 114.4 %all-reduce.11 = (bf16[3,64,1024]{2,1,0:T(8,128)(2,1)}, bf16[64,1024]{1,0:T(8,128)(2,1)}) all-reduce(f32[3,64,1024]{2,1,0:T(8,128)S(1)} %fusion.14, f32[64,1024]{1,0:T(8,128)S(1)} %fusion.9), channel_id=1, replica_groups=mesh['batch'=32,'gy'=4,'gx'=4] {'batch'}, use_global_device_ids=true, to_apply=%region_13.14 | all-reduce | flops 262144 | bytes 1572864 | tf_op jit(solution)/shard_map/psum | solution.py:309
  (140 shorter events, 31.2 us)
Async XLA Ops:
  7.2 69.6 %copy-start = (bf16[3,64,1024]{2,1,0:T(8,128)(2,1)S(1)}, bf16[3,64,1024]{2,1,0:T(8,128)(2,1)}, u32[]{:S(2)}) copy-start(bf16[3,64,1024]{2,1,0:T(8,128)(2,1)} %param.28) | copy-start | bytes 1179652
  7.2 12.9 %copy-start.16 = (bf16[1,4,4,1024]{3,2,1,0:T(4,128)(2,1)S(1)}, bf16[1,4,4,1024]{3,2,1,0:T(4,128)(2,1)}, u32[]{:S(2)}) copy-start(bf16[1,4,4,1024]{3,2,1,0:T(4,128)(2,1)} %param.22) | copy-start | bytes 98308
  10.8 23.3 %copy-start.14 = (bf16[1,4,4,1024]{3,2,1,0:T(4,128)(2,1)S(1)}, bf16[1,4,4,1024]{3,2,1,0:T(4,128)(2,1)}, u32[]{:S(2)}) copy-start(bf16[1,4,4,1024]{3,2,1,0:T(4,128)(2,1)} %param.21) | copy-start | bytes 98308
  12.0 22.2 %copy-start.17 = (f32[1024]{0:T(1024)S(1)}, f32[1024]{0:T(1024)}, u32[]{:S(2)}) copy-start(f32[1024]{0:T(1024)} %param.25) | copy-start | bytes 12292
  12.1 65.7 %collective-permute-start = (bf16[1,3,32,512]{3,2,1,0:T(8,128)(2,1)S(1)}, bf16[1,3,32,512]{3,2,1,0:T(8,128)(2,1)S(1)}, u32[]{:S(2)}, u32[]{:S(2)}) collective-permute-start(bf16[1,3,32,512]{3,2,1,0:T(8,128)(2,1)S(1)} %get-tuple-element.74), channel_id=1, source_target_pairs={{0,4},{4,8},{8,12},{1,5},{5,9},{9,13},{2,6},{6,10},{10,14},{3,7},{... | collective-permute-start | bytes 294920 | tf_op jit(solution)/shard_map/ppermute | solution.py:37
  18.7 59.1 %collective-permute-start.1 = (bf16[1,3,32,512]{3,2,1,0:T(8,128)(2,1)S(1)}, bf16[1,3,32,512]{3,2,1,0:T(8,128)(2,1)S(1)}, u32[]{:S(2)}, u32[]{:S(2)}) collective-permute-start(bf16[1,3,32,512]{3,2,1,0:T(8,128)(2,1)S(1)} %get-tuple-element.75), channel_id=1, source_target_pairs={{4,0},{8,4},{12,8},{5,1},{9,5},{13,9},{6,2},{10,6},{14,10},{7,3},{... | collective-permute-start | bytes 294920 | tf_op jit(solution)/shard_map/ppermute | solution.py:38
  20.9 56.5 %copy-start.9 = (bf16[1,8,32,256]{3,2,1,0:T(8,128)(2,1)S(1)}, bf16[1,8,32,256]{3,2,1,0:T(8,128)(2,1)}, u32[]{:S(2)}) copy-start(bf16[1,8,32,256]{3,2,1,0:T(8,128)(2,1)} %param.20) | copy-start | bytes 393220
  20.9 56.6 %copy-start.13 = (bf16[256,256]{1,0:T(8,128)(2,1)S(1)}, bf16[256,256]{1,0:T(8,128)(2,1)}, u32[]{:S(2)}) copy-start(bf16[256,256]{1,0:T(8,128)(2,1)} %param.27) | copy-start | bytes 393220
  20.9 231.8 %all-to-all-start = ((bf16[16,16,1024]{2,1,0:T(8,128)(2,1)}), bf16[16,16,1024]{2,1,0:T(8,128)(2,1)S(1)}, u32[]{:S(2)}, u32[]{:S(2)}) async-start(bf16[16,16,1024]{2,1,0:T(8,128)(2,1)} %stack.15), calls=%async_computation | async-start | bytes 1048576 | tf_op jit(solution)/shard_map/all_to_all | solution.py:20
  33.9 336.2 %reduce-scatter.2.cloned.1.call-start = ((), (), s32[]{:S(2)}) async-start(), calls=%async_computation.2 | async-start | bytes 557056 | tf_op jit(solution)/shard_map/reduce_scatter | solution.py:304
  77.1 4.9 %copy-start.6 = (bf16[3,256,64]{1,2,0:T(8,128)(2,1)}, bf16[3,256,64]{1,2,0:T(8,128)(2,1)S(1)}, u32[]{:S(2)}) copy-start(bf16[3,256,64]{1,2,0:T(8,128)(2,1)S(1)} %fusion.5) | copy-start | bytes 294916
  77.9 4.5 %collective-permute-start.2 = (bf16[1,14,3,512]{3,2,1,0:T(4,128)(2,1)S(1)}, bf16[1,14,3,512]{3,2,1,0:T(4,128)(2,1)S(1)}, u32[]{:S(2)}, u32[]{:S(2)}) collective-permute-start(bf16[1,14,3,512]{3,2,1,0:T(4,128)(2,1)S(1)} %get-tuple-element.72), channel_id=1, source_target_pairs={{0,1},{1,2},{2,3},{4,5},{5,6},{6,7},{8,9},{9,10},{10,11},{12,13},{... | collective-permute-start | bytes 129032 | tf_op jit(solution)/shard_map/ppermute | solution.py:37
  80.2 5.2 %collective-permute-start.3 = (bf16[1,14,3,512]{3,2,1,0:T(4,128)(2,1)S(1)}, bf16[1,14,3,512]{3,2,1,0:T(4,128)(2,1)S(1)}, u32[]{:S(2)}, u32[]{:S(2)}) collective-permute-start(bf16[1,14,3,512]{3,2,1,0:T(4,128)(2,1)S(1)} %get-tuple-element.73), channel_id=1, source_target_pairs={{1,0},{2,1},{3,2},{5,4},{6,5},{7,6},{9,8},{10,9},{11,10},{13,12},{... | collective-permute-start | bytes 129032 | tf_op jit(solution)/shard_map/ppermute | solution.py:38
  105.0 4.0 %copy-start.10 = (bf16[1,8,32,256]{3,2,1,0:T(8,128)(2,1)S(1)}, bf16[1,8,32,256]{3,2,1,0:T(8,128)(2,1)}, u32[]{:S(2)}) copy-start(bf16[1,8,32,256]{3,2,1,0:T(8,128)(2,1)} %param.20) | copy-start | bytes 393220
  105.0 4.0 %copy-start.11 = (bf16[1,8,4,8,256]{4,3,2,1,0:T(8,128)(2,1)S(1)}, bf16[1,8,4,8,256]{4,3,2,1,0:T(8,128)(2,1)}, u32[]{:S(2)}) copy-start(bf16[1,8,4,8,256]{4,3,2,1,0:T(8,128)(2,1)} %copy.54) | copy-start | bytes 393220
  106.8 8.3 %collective-permute-start.4 = (f32[14,3,512]{2,1,0:T(4,128)}, f32[14,3,512]{2,1,0:T(4,128)}, u32[]{:S(2)}, u32[]{:S(2)}) collective-permute-start(f32[14,3,512]{2,1,0:T(4,128)} %get-tuple-element.63), channel_id=1, source_target_pairs={{0,1},{1,2},{2,3},{4,5},{5,6},{6,7},{8,9},{9,10},{10,11},{12,13},{... | collective-permute-start | bytes 258056 | tf_op jit(solution)/shard_map/ppermute | solution.py:46
  113.8 5.8 %collective-permute-start.5 = (f32[14,3,512]{2,1,0:T(4,128)}, f32[14,3,512]{2,1,0:T(4,128)}, u32[]{:S(2)}, u32[]{:S(2)}) collective-permute-start(f32[14,3,512]{2,1,0:T(4,128)} %get-tuple-element.62), channel_id=1, source_target_pairs={{1,0},{2,1},{3,2},{5,4},{6,5},{7,6},{9,8},{10,9},{11,10},{13,12},{... | collective-permute-start | bytes 258056 | tf_op jit(solution)/shard_map/ppermute | solution.py:46
  116.7 7.4 %copy-start.8 = (bf16[1,4,8,8,256]{4,3,2,1,0:T(8,128)(2,1)S(1)}, bf16[1,4,8,8,256]{4,3,2,1,0:T(8,128)(2,1)}, u32[]{:S(2)}) copy-start(bf16[1,4,8,8,256]{4,3,2,1,0:T(8,128)(2,1)} %reshape_reshape.22) | copy-start | bytes 393220
  120.9 12.2 %copy-start.4 = (bf16[1,8,32,256]{3,2,1,0:T(8,128)(2,1)S(1)}, bf16[1,8,32,256]{3,2,1,0:T(8,128)(2,1)}, u32[]{:S(2)}) copy-start(bf16[1,8,32,256]{3,2,1,0:T(8,128)(2,1)} %param.19) | copy-start | bytes 393220
  120.9 5.6 %collective-permute-start.6 = (f32[3,32,512]{2,1,0:T(8,128)S(1)}, f32[3,32,512]{2,1,0:T(8,128)S(1)}, u32[]{:S(2)}, u32[]{:S(2)}) collective-permute-start(f32[3,32,512]{2,1,0:T(8,128)S(1)} %get-tuple-element.65), channel_id=1, source_target_pairs={{0,4},{4,8},{8,12},{1,5},{5,9},{9,13},{2,6},{6,10},{10,14},{3,7},{... | collective-permute-start | bytes 589832 | tf_op jit(solution)/shard_map/ppermute | solution.py:46
  124.2 8.9 %collective-permute-start.7 = (f32[3,32,512]{2,1,0:T(8,128)S(1)}, f32[3,32,512]{2,1,0:T(8,128)S(1)}, u32[]{:S(2)}, u32[]{:S(2)}) collective-permute-start(f32[3,32,512]{2,1,0:T(8,128)S(1)} %get-tuple-element.64), channel_id=1, source_target_pairs={{4,0},{8,4},{12,8},{5,1},{9,5},{13,9},{6,2},{10,6},{14,10},{7,3},{... | collective-permute-start | bytes 589832 | tf_op jit(solution)/shard_map/ppermute | solution.py:46
  134.1 118.7 %copy-start.15 = (bf16[64,1024]{1,0:T(8,128)(2,1)S(1)}, bf16[64,1024]{1,0:T(8,128)(2,1)}, u32[]{:S(2)}) copy-start(bf16[64,1024]{1,0:T(8,128)(2,1)} %param.29) | copy-start | bytes 393220
  134.5 118.8 %copy-start.7 = (bf16[3,256,64]{1,2,0:T(8,128)(2,1)S(1)}, bf16[3,256,64]{1,2,0:T(8,128)(2,1)}, u32[]{:S(2)}) copy-start(bf16[3,256,64]{1,2,0:T(8,128)(2,1)} %copy-done.6) | copy-start | bytes 294916
  253.6 1.9 copy-start.2
  (4 other events, 4.4 us)
Sparse Core Ops, SparseCore 0:
  255.2 87.0 reduce-scatter.1
